TPU v7x, 32 devices: a whole 2x2x4 slice. The times are simulated.
32 devices in a mesh: row: 4 (over z), col: 2 (over x), rep: 4 (over y, core).
Axes of the slice: x: 2, y: 2, z: 4, core: 2. Of those that a mesh axis runs over, the one named last changes fastest.
Arguments:
- features: bfloat16 [8192, 256], P(('col', 'rep'), 'row'), may hold values from -6 to 6
- weight: bfloat16 [256, 256], replicated, may hold values from -0.375 to 0.375
- cotangent: bfloat16 [8192, 256], P(('row', 'col', 'rep')), may hold values from -6 to 6
- block_values: bfloat16 [4, 8, 128, 128, 128], P('row', ('col', 'rep')), may hold values from -0.0625 to 0.0625
- block_coords: int32 [4, 8, 128, 2], P('row', ('col', 'rep')), may hold values from 0 to 15, as said below
- block_counts: int32 [4, 8], P('row', ('col', 'rep')), may hold values from 1 to 128, as said below
Outputs:
- activations: bfloat16 [8192, 256], P(('row', 'col', 'rep'))
- input_grad: bfloat16 [8192, 256], P(('col', 'rep'), 'row')
- weight_grad: float32 [256, 256], replicated
Inputs may be any that keep to these rules, and one draw needn't show every extreme that they name: `block_coords`: each slot's row block is below 16 and its column block below 8. `block_counts`: some tile uses all 128 slots.
All inputs are finite; a program needn't handle non-finite values.
Results may differ from a plain program's by a relative error of at most 0.014.
Values may be sent and summed in bfloat16 or wider, within the bound.
A program may use at most 128 MiB of HBM per device.

v0:
```python
import math
import jax
import jax.numpy as jnp
from jax import lax
from jax.sharding import PartitionSpec as P


def local(features, weight, cotangent, block_values, block_coords, block_counts):
    blocks = block_values[0, 0]
    coords = block_coords[0, 0]
    live_count = block_counts[0, 0]
    slots = blocks.shape[0]
    gathered = lax.all_gather(features, "row", axis=1, tiled=True)
    feat_width = gathered.shape[1]
    col_blocks = gathered.shape[0] // 128
    row_blocks = cotangent.shape[0] * lax.axis_size(("col", "rep")) // 128
    feat_blocks = gathered.reshape(col_blocks, 128, feat_width)
    is_live = (jnp.arange(slots, dtype=jnp.int32) < live_count).astype(jnp.float32)
    per_turn = math.gcd(slots, 64)
    rounds = slots // per_turn
    pieces = (
        blocks.reshape(rounds, per_turn, 128, 128),
        coords[:, 0].reshape(rounds, per_turn),
        coords[:, 1].reshape(rounds, per_turn),
        is_live.reshape(rounds, per_turn),
    )

    def forward_step(total, piece):
        blocks_g, rows_g, cols_g, live_g = piece
        chosen = feat_blocks[cols_g]
        product = jnp.einsum("bij,bjf->bif", blocks_g, chosen, preferred_element_type=jnp.float32)
        return (total.at[rows_g].add(product * live_g[:, None, None]), None)

    partial_value, _ = lax.scan(
        forward_step, jnp.zeros((row_blocks, 128, feat_width), jnp.float32), pieces
    )
    partial_value = partial_value.reshape(row_blocks * 128, feat_width)
    summed = lax.psum_scatter(partial_value, ("col", "rep"), scatter_dimension=0, tiled=True)
    aggregate = summed.astype(jnp.bfloat16)
    pre_act = jnp.dot(aggregate, weight, preferred_element_type=jnp.float32)
    sigma = jax.nn.sigmoid(pre_act)
    activations = (pre_act * sigma).astype(jnp.bfloat16)
    grad_pre = (cotangent.astype(jnp.float32) * sigma * (1.0 + pre_act * (1.0 - sigma))).astype(
        jnp.bfloat16
    )
    weight_terms = jnp.dot(aggregate.T, grad_pre, preferred_element_type=jnp.float32)
    share = lax.psum_scatter(
        weight_terms.astype(jnp.bfloat16), ("col", "rep"), scatter_dimension=0, tiled=True
    ).astype(jnp.float32)
    share = lax.psum(share, "row")
    weight_grad = lax.all_gather(share, ("col", "rep"), axis=0, tiled=True)
    back_rows = jnp.dot(grad_pre, weight.T, preferred_element_type=jnp.float32).astype(jnp.bfloat16)
    back_all = lax.all_gather(back_rows, ("col", "rep"), axis=0, tiled=True)
    back_blocks = back_all.reshape(row_blocks, 128, back_all.shape[1])

    def backward_step(total, piece):
        blocks_g, rows_g, cols_g, live_g = piece
        chosen = back_blocks[rows_g]
        product = jnp.einsum("bji,bjf->bif", blocks_g, chosen, preferred_element_type=jnp.float32)
        return (total.at[cols_g].add(product * live_g[:, None, None]), None)

    grad_terms, _ = lax.scan(
        backward_step, jnp.zeros((col_blocks, 128, back_all.shape[1]), jnp.float32), pieces
    )
    grad_terms = grad_terms.reshape(col_blocks * 128, back_all.shape[1])
    input_grad = lax.psum_scatter(
        grad_terms.astype(jnp.bfloat16), "row", scatter_dimension=1, tiled=True
    )
    return (activations, input_grad, weight_grad)


def solution(mesh):
    in_specs = (
        P(("col", "rep"), "row"),
        P(),
        P(("row", "col", "rep"), None),
        P("row", ("col", "rep"), None, None, None),
        P("row", ("col", "rep"), None, None),
        P("row", ("col", "rep")),
    )
    out_specs = (P(("row", "col", "rep"), None), P(("col", "rep"), "row"), P())
    return jax.shard_map(local, mesh=mesh, in_specs=in_specs, out_specs=out_specs, check_vma=False)
```

profile of v0, /device:TPU:0, one launch (start us, length us, event | category | flops | bytes accessed | tf_op | source)
XLA Modules:
  0.0 228.0 jit_solution(13461801693741192329)
XLA Ops:
  7.2 0.0 copy-start
  7.2 0.0 reduce-scatter.4.cloned.1.call-start
  7.2 0.8 slice_reduce_fusion
  8.0 0.1 reshape_squeeze.11
  8.1 0.1 reshape_squeeze.9
  8.8 17.6 %all_gather.9 = bf16[1024,256]{0,1:T(8,128)(2,1)S(1)} all-gather(bf16[1024,64]{0,1:T(8,128)(2,1)} %param.10), channel_id=1, replica_groups=mesh['row'=4,'col'=2,'rep'=4] {'row'}, dimensions={1}, use_global_device_ids=true | all-gather | bytes 655360 | tf_op jit(solution)/shard_map/all_gather | solution.py:13
  26.4 0.2 copy.10
  26.6 0.2 broadcast_in_dim.4
  26.8 0.0 copy-start.3
  26.8 45.1 %while.20 = (s32[]{:T(128)}, f32[16,128,256]{2,1,0:T(8,128)S(1)}, s32[2,64]{1,0:T(2,128)S(1)}, bf16[2,64,128,128]{3,2,1,0:T(8,128)(2,1)}, s32[2,64]{1,0:T(2,128)...) while((s32[]{:T(128)}, f32[16,128,256]{2,1,0:T(8,128)S(1)}, ...), condition=%wide.region_2.3_spmd, body=%wide.region_0.2_spmd.sunk | while | flops 541066624 | bytes 48241756 | solution.py:34
  26.9 2.8 %gather_fusion = bf16[64,128,256]{2,1,0:T(8,128)(2,1)} fusion(bf16[8,128,256]{2,1,0:T(8,128)(2,1)S(1)} %get-tuple-element.237, s32[1024]{0:T(1024)S(1)} %pad_clamp_fusion.4), kind=kCustom, calls=%fused_computation.clone.1 | custom fusion | bytes 8388864 | tf_op jit(solution)/shard_map/while/body/eval_jaxpr/gather | solution.py:30
  29.7 7.3 %broadcast_multiply_fusion.4 = f32[64,128,256]{2,1,0:T(8,128)} fusion(f32[64]{0:T(128)S(1)} %fusion.36, bf16[64,128,256]{2,1,0:T(8,128)(2,1)} %gather_fusion, bf16[2,64,128,128]{3,2,1,0:T(8,128)(2,1)} %get-tuple-element.235, s32[]{:T(128)} %get-tuple-element.224), kind=kOutput, calls=%fused_computation.4.clone.1 | convolution fusion | flops 538968064 | bytes 14680832 | tf_op jit(solution)/shard_map/while/body/eval_jaxpr/bij,bjf->bif/dot_general | solution.py:31
  37.0 12.4 %scatter_fusion = f32[16,128,256]{2,1,0:T(8,128)S(1)} fusion(f32[16,128,256]{2,1,0:T(8,128)S(1)} %get-tuple-element.225, s32[64]{0:T(128)S(1)} %get-tuple-element.205, f32[64,128,256]{2,1,0:T(8,128)} %broadcast_multiply_fusion.4), kind=kCustom, calls=%fused_computation.2.clone.1 | custom fusion | flops 2097152 | bytes 25166080 | tf_op jit(solution)/shard_map/while/body/eval_jaxpr/scatter-add | solution.py:32
  49.4 2.8 %gather_fusion = bf16[64,128,256]{2,1,0:T(8,128)(2,1)} fusion(bf16[8,128,256]{2,1,0:T(8,128)(2,1)S(1)} %get-tuple-element.237, s32[1024]{0:T(1024)S(1)} %pad_clamp_fusion.4), kind=kCustom, calls=%fused_computation.clone.1 | custom fusion | bytes 8388864 | tf_op jit(solution)/shard_map/while/body/eval_jaxpr/gather | solution.py:30
  52.2 7.3 %broadcast_multiply_fusion.4 = f32[64,128,256]{2,1,0:T(8,128)} fusion(f32[64]{0:T(128)S(1)} %fusion.36, bf16[64,128,256]{2,1,0:T(8,128)(2,1)} %gather_fusion, bf16[2,64,128,128]{3,2,1,0:T(8,128)(2,1)} %get-tuple-element.235, s32[]{:T(128)} %get-tuple-element.224), kind=kOutput, calls=%fused_computation.4.clone.1 | convolution fusion | flops 538968064 | bytes 14680832 | tf_op jit(solution)/shard_map/while/body/eval_jaxpr/bij,bjf->bif/dot_general | solution.py:31
  59.5 12.4 %scatter_fusion = f32[16,128,256]{2,1,0:T(8,128)S(1)} fusion(f32[16,128,256]{2,1,0:T(8,128)S(1)} %get-tuple-element.225, s32[64]{0:T(128)S(1)} %get-tuple-element.205, f32[64,128,256]{2,1,0:T(8,128)} %broadcast_multiply_fusion.4), kind=kCustom, calls=%fused_computation.2.clone.1 | custom fusion | flops 2097152 | bytes 25166080 | tf_op jit(solution)/shard_map/while/body/eval_jaxpr/scatter-add | solution.py:32
  71.9 0.0 copy-start.1
  72.0 1.3 copy-done.1
  73.3 0.0 reduce-scatter.4.cloned.1.call-update
  73.3 0.0 all-gather.2.cloned.1.call-start
  73.4 43.0 %reduce-scatter.4.cloned.1.call-done = f32[256,256]{1,0:T(8,128)} async-done(((f32[2048,256]{1,0:T(8,128)}), f32[256,256]{1,0:T(8,128)}) %reduce-scatter.4.cloned.1.call-update) | async-done | bytes 262160 | tf_op jit(solution)/shard_map/reduce_scatter | solution.py:38
  116.4 0.0 copy-done
  116.4 0.0 copy-done.3
  116.4 1.9 multiply_convert_fusion
  118.3 0.9 convolution_convert_fusion.1
  119.2 0.0 all-gather.2.cloned.1.call-update
  119.2 0.0 copy-start.2
  119.2 0.0 reduce-scatter.8.cloned.1.call-start
  119.2 6.4 %copy.9 = bf16[1,1,128,128,128]{3,4,2,1,0:T(8,128)(2,1)} copy(bf16[1,1,128,128,128]{4,3,2,1,0:T(8,128)(2,1)} %bitcast.81) | data formatting | bytes 8388608 | tf_op args[3]
  125.6 0.0 copy-done.2
  125.6 0.9 convolution_convert_fusion
  126.5 0.0 reduce-scatter.8.cloned.1.call-update
  126.5 0.0 reduce-scatter.6.cloned.1.call-start
  126.6 16.1 %all-gather.2.cloned.1.call-done = bf16[2048,256]{1,0:T(8,128)(2,1)} async-done(((bf16[256,256]{1,0:T(8,128)(2,1)}), bf16[2048,256]{1,0:T(8,128)(2,1)}) %all-gather.2.cloned.1.call-update) | async-done | bytes 1048592 | tf_op jit(solution)/shard_map/all_gather | solution.py:53
  142.7 0.1 broadcast_in_dim.8
  142.8 47.4 %while.21 = (s32[]{:T(128)}, f32[8,128,256]{2,1,0:T(8,128)S(1)}, s32[2,64]{1,0:T(2,128)S(1)}, bf16[2,64,128,128]{2,3,1,0:T(8,128)(2,1)}, s32[2,64]{1,0:T(2,128)S...) while((s32[]{:T(128)}, f32[8,128,256]{2,1,0:T(8,128)S(1)}, s32[2,64]{1,0:T(2,128)S(1)}, ...), condition=%wide.region_6.7_spmd, body=%wide.region_4.6_spmd.sunk | while | flops 541066624 | bytes 48241756 | solution.py:62
  142.8 4.0 %gather_fusion.1 = bf16[64,128,256]{2,1,0:T(8,128)(2,1)} fusion(bf16[16,128,256]{2,1,0:T(8,128)(2,1)} %get-tuple-element.261, s32[1024]{0:T(1024)S(1)} %pad_clamp_fusion.5), kind=kCustom, calls=%fused_computation.1.clone.1 | custom fusion | bytes 8388864 | tf_op jit(solution)/shard_map/while/body/eval_jaxpr/gather | solution.py:58
  146.8 7.3 %broadcast_multiply_fusion.5 = f32[64,128,256]{2,1,0:T(8,128)} fusion(f32[64]{0:T(128)S(1)} %fusion.40, bf16[64,128,256]{2,1,0:T(8,128)(2,1)} %gather_fusion.1, bf16[2,64,128,128]{2,3,1,0:T(8,128)(2,1)} %get-tuple-element.259, s32[]{:T(128)} %get-tuple-element.248), kind=kOutput, calls=%fused_computation.19.clone.1 | convolution fusion | flops 538968064 | bytes 14680832 | tf_op jit(solution)/shard_map/while/body/eval_jaxpr/bji,bjf->bif/dot_general | solution.py:59
  154.1 12.4 %scatter_fusion.1 = f32[8,128,256]{2,1,0:T(8,128)S(1)} fusion(f32[8,128,256]{2,1,0:T(8,128)S(1)} %get-tuple-element.249, s32[64]{0:T(128)S(1)} %get-tuple-element.214, f32[64,128,256]{2,1,0:T(8,128)} %broadcast_multiply_fusion.5), kind=kCustom, calls=%fused_computation.3.clone.1 | custom fusion | flops 2097152 | bytes 25166080 | tf_op jit(solution)/shard_map/while/body/eval_jaxpr/scatter-add | solution.py:60
  166.5 4.0 %gather_fusion.1 = bf16[64,128,256]{2,1,0:T(8,128)(2,1)} fusion(bf16[16,128,256]{2,1,0:T(8,128)(2,1)} %get-tuple-element.261, s32[1024]{0:T(1024)S(1)} %pad_clamp_fusion.5), kind=kCustom, calls=%fused_computation.1.clone.1 | custom fusion | bytes 8388864 | tf_op jit(solution)/shard_map/while/body/eval_jaxpr/gather | solution.py:58
  170.6 7.3 %broadcast_multiply_fusion.5 = f32[64,128,256]{2,1,0:T(8,128)} fusion(f32[64]{0:T(128)S(1)} %fusion.40, bf16[64,128,256]{2,1,0:T(8,128)(2,1)} %gather_fusion.1, bf16[2,64,128,128]{2,3,1,0:T(8,128)(2,1)} %get-tuple-element.259, s32[]{:T(128)} %get-tuple-element.248), kind=kOutput, calls=%fused_computation.19.clone.1 | convolution fusion | flops 538968064 | bytes 14680832 | tf_op jit(solution)/shard_map/while/body/eval_jaxpr/bji,bjf->bif/dot_general | solution.py:59
  177.8 12.4 %scatter_fusion.1 = f32[8,128,256]{2,1,0:T(8,128)S(1)} fusion(f32[8,128,256]{2,1,0:T(8,128)S(1)} %get-tuple-element.249, s32[64]{0:T(128)S(1)} %get-tuple-element.214, f32[64,128,256]{2,1,0:T(8,128)} %broadcast_multiply_fusion.5), kind=kCustom, calls=%fused_computation.3.clone.1 | custom fusion | flops 2097152 | bytes 25166080 | tf_op jit(solution)/shard_map/while/body/eval_jaxpr/scatter-add | solution.py:60
  190.2 0.1 convert_element_type.37
  190.3 1.0 copy.14
  191.3 0.0 reduce-scatter.6.cloned.1.call-update
  191.3 0.0 reduce-scatter.8.cloned.1.call-done
  191.4 20.2 %psum.7 = f32[32,256]{1,0:T(8,128)S(1)} all-reduce(bf16[32,256]{1,0:T(8,128)(2,1)} %reduce-scatter.8.cloned.1.call-done), channel_id=1, replica_groups=mesh['row'=4,'col'=2,'rep'=4] {'row'}, use_global_device_ids=true, to_apply=%region_9.10 | all-reduce | flops 8192 | bytes 49152 | tf_op jit(solution)/shard_map/psum | solution.py:50
  211.6 9.2 %all_gather.11 = f32[256,256]{1,0:T(8,128)S(1)} all-gather(f32[32,256]{1,0:T(8,128)S(1)} %psum.7), channel_id=1, replica_groups=mesh['row'=4,'col'=2,'rep'=4] {'col','rep'}, dimensions={0}, use_global_device_ids=true | all-gather | bytes 294912 | tf_op jit(solution)/shard_map/all_gather | solution.py:51
  220.8 0.0 reduce-scatter.6.cloned.1.call-done
  220.8 0.7 copy.33
  (13 shorter events, 0.1 us)
Async XLA Ops:
  7.2 109.2 %copy-start = (bf16[256,256]{1,0:T(8,128)(2,1)S(1)}, bf16[256,256]{1,0:T(8,128)(2,1)}, u32[]{:S(2)}) copy-start(bf16[256,256]{1,0:T(8,128)(2,1)} %param.11) | copy-start | bytes 393220
  7.2 109.2 %reduce-scatter.4.cloned.1.call-start = ((), (), s32[]{:S(2)}) async-start(), calls=%async_computation.3 | async-start | bytes 2359296 | tf_op jit(solution)/shard_map/reduce_scatter | solution.py:38
  26.8 89.6 %copy-start.3 = (bf16[256,256]{1,0:T(8,128)(2,1)S(1)}, bf16[256,256]{1,0:T(8,128)(2,1)}, u32[]{:S(2)}) copy-start(bf16[256,256]{1,0:T(8,128)(2,1)} %param.12) | copy-start | bytes 393220
  71.9 1.4 copy-start.1
  73.3 69.4 %all-gather.2.cloned.1.call-start = ((), (), s32[]{:S(2)}) async-start(), calls=%async_computation.4 | async-start | bytes 1179648 | tf_op jit(solution)/shard_map/all_gather | solution.py:53
  119.2 6.5 %copy-start.2 = (f32[256,256]{1,0:T(8,128)S(1)}, f32[256,256]{1,0:T(8,128)}, u32[]{:S(2)}) copy-start(f32[256,256]{1,0:T(8,128)} %reduce-scatter.4.cloned.1.call-done) | copy-start | bytes 786436
  119.2 72.1 %reduce-scatter.8.cloned.1.call-start = ((), (), s32[]{:S(2)}) async-start(), calls=%async_computation.6 | async-start | bytes 147456 | tf_op jit(solution)/shard_map/reduce_scatter | solution.py:47
  126.5 94.3 %reduce-scatter.6.cloned.1.call-start = ((), (), s32[]{:S(2)}) async-start(), calls=%async_computation.5 | async-start | bytes 655360 | tf_op jit(solution)/shard_map/reduce_scatter | solution.py:66
Sparse Core Ops, SparseCore 0:
  73.4 42.9 reduce-scatter.3
  119.3 23.3 all-gather.1
  146.3 33.5 reduce-scatter.7
  191.4 22.2 reduce-scatter.5
where the time goes:
time: 229 us; the launch traced here: 228 us
  waiting for transfers between devices  59.2 us (26%)
  other arithmetic  49.7 us (22%)
  blocking collectives  47 us (21%)
  matrix products  32.8 us (14%)
  local copies, waits for them, and re-layouts  24.5 us (11%)
  between operations  14.5 us (6%)
    reduce_scatter x1, waiting for transfers between devices, local(): lax.psum_scatter(partial_value, ('col', 'rep'), scatter_dimension=0, tile...  43 us
    scatter-add x2, other arithmetic, forward_step(): return (total.at[rows_g].add(product * live_g[:, None, None]), None)  24.8 us
    scatter-add x2, other arithmetic, backward_step(): return (total.at[cols_g].add(product * live_g[:, None, None]), None)  24.8 us
    psum x1, blocking collectives, local(): share = lax.psum(share, 'row')  20.2 us
    all_gather x1, blocking collectives, local(): gathered = lax.all_gather(features, 'row', axis=1, tiled=True)  17.6 us
    all_gather x1, waiting for transfers between devices, local(): back_all = lax.all_gather(back_rows, ('col', 'rep'), axis=0, tiled=True)  16.1 us
    dot_general x2, matrix products, forward_step(): jnp.einsum('bij,bjf->bif', blocks_g, chosen, preferred_element_type=jnp.f...  14.6 us
    dot_general x2, matrix products, backward_step(): jnp.einsum('bji,bjf->bif', blocks_g, chosen, preferred_element_type=jnp.f...  14.6 us
  transfers between devices with their start and end apart: 4, of which 2 were waited for; matrix products, arithmetic and copies ran while one was open for 24% of the time, Pallas kernels for 0%

commit v1 on v0

--- a/solution.py
+++ b/solution.py
@@ -3,6 +3,20 @@
 import jax.numpy as jnp
 from jax import lax
 from jax.sharding import PartitionSpec as P
+from jax.lax import ppermute, psum
+
+
+def _divide_records(vals):
+    amount_of = psum(1, axis_name="row")
+    current_block, right_arr = (vals, 0)
+    while 1 << right_arr < amount_of:
+        r1 = range(amount_of)
+        a_now = map(lambda jj: (jj, jj ^ 1 << right_arr), r1)
+        v_next = list(a_now)
+        item_now = ppermute(current_block, axis_name="row", perm=v_next)
+        current_block = current_block + item_now
+        right_arr = right_arr + 1
+    return current_block
 
 
 def local(features, weight, cotangent, block_values, block_coords, block_counts):
@@ -47,7 +61,7 @@
     share = lax.psum_scatter(
         weight_terms.astype(jnp.bfloat16), ("col", "rep"), scatter_dimension=0, tiled=True
     ).astype(jnp.float32)
-    share = lax.psum(share, "row")
+    share = _divide_records(share)
     weight_grad = lax.all_gather(share, ("col", "rep"), axis=0, tiled=True)
     back_rows = jnp.dot(grad_pre, weight.T, preferred_element_type=jnp.float32).astype(jnp.bfloat16)
     back_all = lax.all_gather(back_rows, ("col", "rep"), axis=0, tiled=True)

time: 229 us -> 222 us (0.969)
  blocking collectives: 47 us -> 26.8 us
  waiting for transfers between devices: 59.2 us -> 66.9 us
  starting transfers between devices: 0.16 us -> 4.06 us
    psum x1 -> x0, blocking collectives: 20.2 us -> none  [local(): share = lax.psum(share, 'row')]
    ppermute x0 -> x2, waiting for transfers between devices: none -> 6.57 us  [_divide_records(): item_now = ppermute(current_block, axis_name='row', perm=v_next)]
    ppermute x0 -> x2, starting transfers between devices: none -> 3.9 us  [_divide_records(): item_now = ppermute(current_block, axis_name='row', perm=v_next)]
  transfers between devices with their start and end apart: 4 -> 6, of which waited for: 2 -> 5; matrix products, arithmetic and copies ran while one was open for 24% -> 26% of each run, Pallas kernels for 0% -> 0%
where the time goes in v1:
time: 222 us; the launch traced here: 221 us
  waiting for transfers between devices  66.9 us (30%)
  other arithmetic  51.2 us (23%)
  matrix products  32.8 us (15%)
  blocking collectives  26.8 us (12%)
  local copies, waits for them, and re-layouts  24.4 us (11%)
  between operations  14.5 us (7%)
  starting transfers between devices  4.06 us (2%)
    reduce_scatter x1, waiting for transfers between devices, local(): lax.psum_scatter(partial_value, ('col', 'rep'), scatter_dimension=0, tile...  43 us
    scatter-add x2, other arithmetic, forward_step(): return (total.at[rows_g].add(product * live_g[:, None, None]), None)  24.8 us
    scatter-add x2, other arithmetic, backward_step(): return (total.at[cols_g].add(product * live_g[:, None, None]), None)  24.8 us
    all_gather x1, blocking collectives, local(): gathered = lax.all_gather(features, 'row', axis=1, tiled=True)  17.6 us
    all_gather x1, waiting for transfers between devices, local(): back_all = lax.all_gather(back_rows, ('col', 'rep'), axis=0, tiled=True)  16.1 us
    dot_general x2, matrix products, backward_step(): jnp.einsum('bji,bjf->bif', blocks_g, chosen, preferred_element_type=jnp.f...  14.6 us
    dot_general x2, matrix products, forward_step(): jnp.einsum('bij,bjf->bif', blocks_g, chosen, preferred_element_type=jnp.f...  14.6 us
    all_gather x1, blocking collectives, local(): weight_grad = lax.all_gather(share, ('col', 'rep'), axis=0, tiled=True)  9.21 us
  transfers between devices with their start and end apart: 6, of which 5 were waited for; matrix products, arithmetic and copies ran while one was open for 26% of the time, Pallas kernels for 0%

profile of v1, /device:TPU:0, one launch (start us, length us, event | category | flops | bytes accessed | tf_op | source)
XLA Modules:
  0.0 220.8 jit_solution(10059310440463415122)
XLA Ops:
  7.2 0.0 copy-start
  7.2 0.0 reduce-scatter.4.cloned.1.call-start
  7.2 0.8 slice_reduce_fusion
  8.0 0.1 reshape_squeeze.11
  8.1 0.1 reshape_squeeze.9
  8.8 17.6 %all_gather.9 = bf16[1024,256]{0,1:T(8,128)(2,1)S(1)} all-gather(bf16[1024,64]{0,1:T(8,128)(2,1)} %param.10), channel_id=1, replica_groups=mesh['row'=4,'col'=2,'rep'=4] {'row'}, dimensions={1}, use_global_device_ids=true | all-gather | bytes 655360 | tf_op jit(solution)/shard_map/all_gather | solution.py:27
  26.4 0.2 copy.10
  26.6 0.2 broadcast_in_dim.4
  26.8 0.0 copy-start.3
  26.8 45.0 %while.20 = (s32[]{:T(128)}, f32[16,128,256]{2,1,0:T(8,128)S(1)}, s32[2,64]{1,0:T(2,128)S(1)}, bf16[2,64,128,128]{3,2,1,0:T(8,128)(2,1)}, s32[2,64]{1,0:T(2,128)...) while((s32[]{:T(128)}, f32[16,128,256]{2,1,0:T(8,128)S(1)}, ...), condition=%wide.region_2.3_spmd, body=%wide.region_0.2_spmd.sunk | while | flops 541066624 | bytes 48241756 | solution.py:48
  26.9 2.8 %gather_fusion = bf16[64,128,256]{2,1,0:T(8,128)(2,1)} fusion(bf16[8,128,256]{2,1,0:T(8,128)(2,1)S(1)} %get-tuple-element.237, s32[1024]{0:T(1024)S(1)} %pad_clamp_fusion.4), kind=kCustom, calls=%fused_computation.clone.1 | custom fusion | bytes 8388864 | tf_op jit(solution)/shard_map/while/body/eval_jaxpr/gather | solution.py:44
  29.6 7.3 %broadcast_multiply_fusion.4 = f32[64,128,256]{2,1,0:T(8,128)} fusion(f32[64]{0:T(128)S(1)} %fusion.36, bf16[64,128,256]{2,1,0:T(8,128)(2,1)} %gather_fusion, bf16[2,64,128,128]{3,2,1,0:T(8,128)(2,1)} %get-tuple-element.235, s32[]{:T(128)} %get-tuple-element.224), kind=kOutput, calls=%fused_computation.4.clone.1 | convolution fusion | flops 538968064 | bytes 14680832 | tf_op jit(solution)/shard_map/while/body/eval_jaxpr/bij,bjf->bif/dot_general | solution.py:45
  36.9 12.4 %scatter_fusion = f32[16,128,256]{2,1,0:T(8,128)S(1)} fusion(f32[16,128,256]{2,1,0:T(8,128)S(1)} %get-tuple-element.225, s32[64]{0:T(128)S(1)} %get-tuple-element.205, f32[64,128,256]{2,1,0:T(8,128)} %broadcast_multiply_fusion.4), kind=kCustom, calls=%fused_computation.2.clone.1 | custom fusion | flops 2097152 | bytes 25166080 | tf_op jit(solution)/shard_map/while/body/eval_jaxpr/scatter-add | solution.py:46
  49.4 2.8 %gather_fusion = bf16[64,128,256]{2,1,0:T(8,128)(2,1)} fusion(bf16[8,128,256]{2,1,0:T(8,128)(2,1)S(1)} %get-tuple-element.237, s32[1024]{0:T(1024)S(1)} %pad_clamp_fusion.4), kind=kCustom, calls=%fused_computation.clone.1 | custom fusion | bytes 8388864 | tf_op jit(solution)/shard_map/while/body/eval_jaxpr/gather | solution.py:44
  52.2 7.3 %broadcast_multiply_fusion.4 = f32[64,128,256]{2,1,0:T(8,128)} fusion(f32[64]{0:T(128)S(1)} %fusion.36, bf16[64,128,256]{2,1,0:T(8,128)(2,1)} %gather_fusion, bf16[2,64,128,128]{3,2,1,0:T(8,128)(2,1)} %get-tuple-element.235, s32[]{:T(128)} %get-tuple-element.224), kind=kOutput, calls=%fused_computation.4.clone.1 | convolution fusion | flops 538968064 | bytes 14680832 | tf_op jit(solution)/shard_map/while/body/eval_jaxpr/bij,bjf->bif/dot_general | solution.py:45
  59.5 12.4 %scatter_fusion = f32[16,128,256]{2,1,0:T(8,128)S(1)} fusion(f32[16,128,256]{2,1,0:T(8,128)S(1)} %get-tuple-element.225, s32[64]{0:T(128)S(1)} %get-tuple-element.205, f32[64,128,256]{2,1,0:T(8,128)} %broadcast_multiply_fusion.4), kind=kCustom, calls=%fused_computation.2.clone.1 | custom fusion | flops 2097152 | bytes 25166080 | tf_op jit(solution)/shard_map/while/body/eval_jaxpr/scatter-add | solution.py:46
  71.9 0.0 copy-start.1
  71.9 1.3 copy-done.1
  73.2 0.0 reduce-scatter.4.cloned.1.call-update
  73.2 0.0 all-gather.2.cloned.1.call-start
  73.3 43.0 %reduce-scatter.4.cloned.1.call-done = f32[256,256]{1,0:T(8,128)} async-done(((f32[2048,256]{1,0:T(8,128)}), f32[256,256]{1,0:T(8,128)}) %reduce-scatter.4.cloned.1.call-update) | async-done | bytes 262160 | tf_op jit(solution)/shard_map/reduce_scatter | solution.py:52
  116.3 0.0 copy-done
  116.3 0.0 copy-done.3
  116.3 1.9 multiply_convert_fusion
  118.2 0.9 convolution_convert_fusion.1
  119.1 0.0 all-gather.2.cloned.1.call-update
  119.1 0.0 copy-start.2
  119.1 0.0 reduce-scatter.8.cloned.1.call-start
  119.2 6.4 %copy.9 = bf16[1,1,128,128,128]{3,4,2,1,0:T(8,128)(2,1)} copy(bf16[1,1,128,128,128]{4,3,2,1,0:T(8,128)(2,1)} %bitcast.81) | data formatting | bytes 8388608 | tf_op args[3]
  125.6 0.0 copy-done.2
  125.6 0.9 convolution_convert_fusion
  126.4 0.0 reduce-scatter.8.cloned.1.call-update
  126.5 0.0 reduce-scatter.6.cloned.1.call-start
  126.5 16.1 %all-gather.2.cloned.1.call-done = bf16[2048,256]{1,0:T(8,128)(2,1)} async-done(((bf16[256,256]{1,0:T(8,128)(2,1)}), bf16[2048,256]{1,0:T(8,128)(2,1)}) %all-gather.2.cloned.1.call-update) | async-done | bytes 1048592 | tf_op jit(solution)/shard_map/all_gather | solution.py:67
  142.6 0.1 broadcast_in_dim.8
  142.7 47.4 %while.21 = (s32[]{:T(128)}, f32[8,128,256]{2,1,0:T(8,128)S(1)}, s32[2,64]{1,0:T(2,128)S(1)}, bf16[2,64,128,128]{2,3,1,0:T(8,128)(2,1)}, s32[2,64]{1,0:T(2,128)S...) while((s32[]{:T(128)}, f32[8,128,256]{2,1,0:T(8,128)S(1)}, s32[2,64]{1,0:T(2,128)S(1)}, ...), condition=%wide.region_6.7_spmd, body=%wide.region_4.6_spmd.sunk | while | flops 541066624 | bytes 48241756 | solution.py:76
  142.7 4.0 %gather_fusion.1 = bf16[64,128,256]{2,1,0:T(8,128)(2,1)} fusion(bf16[16,128,256]{2,1,0:T(8,128)(2,1)} %get-tuple-element.261, s32[1024]{0:T(1024)S(1)} %pad_clamp_fusion.5), kind=kCustom, calls=%fused_computation.1.clone.1 | custom fusion | bytes 8388864 | tf_op jit(solution)/shard_map/while/body/eval_jaxpr/gather | solution.py:72
  146.7 7.3 %broadcast_multiply_fusion.5 = f32[64,128,256]{2,1,0:T(8,128)} fusion(f32[64]{0:T(128)S(1)} %fusion.40, bf16[64,128,256]{2,1,0:T(8,128)(2,1)} %gather_fusion.1, bf16[2,64,128,128]{2,3,1,0:T(8,128)(2,1)} %get-tuple-element.259, s32[]{:T(128)} %get-tuple-element.248), kind=kOutput, calls=%fused_computation.19.clone.1 | convolution fusion | flops 538968064 | bytes 14680832 | tf_op jit(solution)/shard_map/while/body/eval_jaxpr/bji,bjf->bif/dot_general | solution.py:73
  154.0 12.4 %scatter_fusion.1 = f32[8,128,256]{2,1,0:T(8,128)S(1)} fusion(f32[8,128,256]{2,1,0:T(8,128)S(1)} %get-tuple-element.249, s32[64]{0:T(128)S(1)} %get-tuple-element.214, f32[64,128,256]{2,1,0:T(8,128)} %broadcast_multiply_fusion.5), kind=kCustom, calls=%fused_computation.3.clone.1 | custom fusion | flops 2097152 | bytes 25166080 | tf_op jit(solution)/shard_map/while/body/eval_jaxpr/scatter-add | solution.py:74
  166.4 4.0 %gather_fusion.1 = bf16[64,128,256]{2,1,0:T(8,128)(2,1)} fusion(bf16[16,128,256]{2,1,0:T(8,128)(2,1)} %get-tuple-element.261, s32[1024]{0:T(1024)S(1)} %pad_clamp_fusion.5), kind=kCustom, calls=%fused_computation.1.clone.1 | custom fusion | bytes 8388864 | tf_op jit(solution)/shard_map/while/body/eval_jaxpr/gather | solution.py:72
  170.4 7.3 %broadcast_multiply_fusion.5 = f32[64,128,256]{2,1,0:T(8,128)} fusion(f32[64]{0:T(128)S(1)} %fusion.40, bf16[64,128,256]{2,1,0:T(8,128)(2,1)} %gather_fusion.1, bf16[2,64,128,128]{2,3,1,0:T(8,128)(2,1)} %get-tuple-element.259, s32[]{:T(128)} %get-tuple-element.248), kind=kOutput, calls=%fused_computation.19.clone.1 | convolution fusion | flops 538968064 | bytes 14680832 | tf_op jit(solution)/shard_map/while/body/eval_jaxpr/bji,bjf->bif/dot_general | solution.py:73
  177.7 12.4 %scatter_fusion.1 = f32[8,128,256]{2,1,0:T(8,128)S(1)} fusion(f32[8,128,256]{2,1,0:T(8,128)S(1)} %get-tuple-element.249, s32[64]{0:T(128)S(1)} %get-tuple-element.214, f32[64,128,256]{2,1,0:T(8,128)} %broadcast_multiply_fusion.5), kind=kCustom, calls=%fused_computation.3.clone.1 | custom fusion | flops 2097152 | bytes 25166080 | tf_op jit(solution)/shard_map/while/body/eval_jaxpr/scatter-add | solution.py:74
  190.1 0.1 convert_element_type.37
  190.2 1.0 copy.14
  191.2 0.0 reduce-scatter.6.cloned.1.call-update
  191.2 0.0 reduce-scatter.8.cloned.1.call-done
  191.2 0.7 convert_element_type.40
  191.9 1.5 collective-permute-start
  193.4 2.4 %collective-permute-done = f32[32,256]{1,0:T(8,128)S(1)} collective-permute-done((f32[32,256]{1,0:T(8,128)S(1)}, f32[32,256]{1,0:T(8,128)S(1)}, u32[]{:S(2)}, u32[]{:S(2)}) %collective-permute-start) | collective-permute-done | bytes 32800 | tf_op jit(solution)/shard_map/ppermute | solution.py:16
  195.9 0.7 convert_add_fusion
  196.6 2.4 %collective-permute-start.1 = (f32[32,256]{1,0:T(8,128)S(1)}, f32[32,256]{1,0:T(8,128)S(1)}, u32[]{:S(2)}, u32[]{:S(2)}) collective-permute-start(f32[32,256]{1,0:T(8,128)S(1)} %convert_add_fusion), channel_id=1, source_target_pairs={{0,16},{8,24},{16,0},{24,8},{1,17},{9,25},{17,1},{25,9},{2,18},{10... | collective-permute-start | bytes 98312 | tf_op jit(solution)/shard_map/ppermute | solution.py:16
  199.0 4.1 %collective-permute-done.1 = f32[32,256]{1,0:T(8,128)S(1)} collective-permute-done((f32[32,256]{1,0:T(8,128)S(1)}, f32[32,256]{1,0:T(8,128)S(1)}, u32[]{:S(2)}, u32[]{:S(2)}) %collective-permute-start.1) | collective-permute-done | bytes 32800 | tf_op jit(solution)/shard_map/ppermute | solution.py:16
  203.1 9.2 %all_gather.11 = f32[256,256]{1,0:T(8,128)S(1)} all-gather(f32[32,256]{1,0:T(8,128)S(1)} %add.72), channel_id=1, replica_groups=mesh['row'=4,'col'=2,'rep'=4] {'col','rep'}, dimensions={0}, use_global_device_ids=true | all-gather | bytes 294912 | tf_op jit(solution)/shard_map/all_gather | solution.py:65
  212.4 1.2 reduce-scatter.6.cloned.1.call-done
  213.5 0.7 copy.33
  (14 shorter events, 0.1 us)
Async XLA Ops:
  7.2 109.1 %copy-start = (bf16[256,256]{1,0:T(8,128)(2,1)S(1)}, bf16[256,256]{1,0:T(8,128)(2,1)}, u32[]{:S(2)}) copy-start(bf16[256,256]{1,0:T(8,128)(2,1)} %param.11) | copy-start | bytes 393220
  7.2 109.1 %reduce-scatter.4.cloned.1.call-start = ((), (), s32[]{:S(2)}) async-start(), calls=%async_computation.3 | async-start | bytes 2359296 | tf_op jit(solution)/shard_map/reduce_scatter | solution.py:52
  26.8 89.5 %copy-start.3 = (bf16[256,256]{1,0:T(8,128)(2,1)S(1)}, bf16[256,256]{1,0:T(8,128)(2,1)}, u32[]{:S(2)}) copy-start(bf16[256,256]{1,0:T(8,128)(2,1)} %param.12) | copy-start | bytes 393220
  71.9 1.3 copy-start.1
  73.2 69.4 %all-gather.2.cloned.1.call-start = ((), (), s32[]{:S(2)}) async-start(), calls=%async_computation.4 | async-start | bytes 1179648 | tf_op jit(solution)/shard_map/all_gather | solution.py:67
  119.1 6.5 %copy-start.2 = (f32[256,256]{1,0:T(8,128)S(1)}, f32[256,256]{1,0:T(8,128)}, u32[]{:S(2)}) copy-start(f32[256,256]{1,0:T(8,128)} %reduce-scatter.4.cloned.1.call-done) | copy-start | bytes 786436
  119.1 72.1 %reduce-scatter.8.cloned.1.call-start = ((), (), s32[]{:S(2)}) async-start(), calls=%async_computation.6 | async-start | bytes 147456 | tf_op jit(solution)/shard_map/reduce_scatter | solution.py:61
  126.5 87.1 %reduce-scatter.6.cloned.1.call-start = ((), (), s32[]{:S(2)}) async-start(), calls=%async_computation.5 | async-start | bytes 655360 | tf_op jit(solution)/shard_map/reduce_scatter | solution.py:80
  191.9 3.9 %collective-permute-start = (f32[32,256]{1,0:T(8,128)S(1)}, f32[32,256]{1,0:T(8,128)S(1)}, u32[]{:S(2)}, u32[]{:S(2)}) collective-permute-start(f32[32,256]{1,0:T(8,128)S(1)} %convert_element_type.40), channel_id=1, source_target_pairs={{0,8},{8,0},{16,24},{24,16},{1,9},{9,1},{17,25},{25,17},{2,10},{10... | collective-permute-start | bytes 98312 | tf_op jit(solution)/shard_map/ppermute | solution.py:16
  196.6 6.6 %collective-permute-start.1 = (f32[32,256]{1,0:T(8,128)S(1)}, f32[32,256]{1,0:T(8,128)S(1)}, u32[]{:S(2)}, u32[]{:S(2)}) collective-permute-start(f32[32,256]{1,0:T(8,128)S(1)} %convert_add_fusion), channel_id=1, source_target_pairs={{0,16},{8,24},{16,0},{24,8},{1,17},{9,25},{17,1},{25,9},{2,18},{10... | collective-permute-start | bytes 98312 | tf_op jit(solution)/shard_map/ppermute | solution.py:16
Sparse Core Ops, SparseCore 0:
  73.4 42.9 reduce-scatter.3
  119.2 23.3 all-gather.1
  146.2 33.5 reduce-scatter.7
  191.3 22.1 reduce-scatter.5
